TPU v7x, 32 devices: a whole 2x2x4 slice. The times are simulated.
32 devices in a mesh: dp: 2 (over x), layer: 4 (over y, core), tensor: 4 (over z).
Axes of the slice: x: 2, y: 2, z: 4, core: 2. Of those that a mesh axis runs over, the one named last changes fastest.
Arguments:
- embeddings: bfloat16 [256, 4096], P('dp', 'tensor'), may hold values from -180 to 180
- layer_weight: bfloat16 [8, 4096, 4096], P('layer', None, 'tensor'), may hold values from -0.09375 to 0.09375
- rotation: float32 [4096, 4096], P(('dp', 'layer'), 'tensor'), may hold values from -3.2 to 3.2
Outputs:
- updated_rotation: float32 [4096, 4096], P(('dp', 'layer'), 'tensor')
All inputs are finite; a program needn't handle non-finite values.
Results may differ from a plain program's by a relative error of at most 0.0042.
Values may be sent and summed in bfloat16 or wider, within the bound.
A program may use at most 128 MiB of HBM per device.

v0:
```python
import math
import jax
import jax.numpy as jnp
from jax import lax
from jax.sharding import PartitionSpec as P

D = 4096
MICRO = 4


def passed_along(value, axis, steps):
    count = lax.axis_size(axis)
    initial, last = (max(0, -steps), min(count, count - steps))
    return lax.ppermute(value, axis, [(source, source + steps) for source in range(initial, last)])


def normalize(hidden):
    widened = hidden.astype(jnp.float32)
    inverse = lax.rsqrt(jnp.mean(widened * widened, axis=-1, keepdims=True) + 1e-05)
    return (widened, (widened * inverse).astype(jnp.bfloat16))


def shards(embeddings, layer_weight, rotation):
    exact_mode = lax.Precision.HIGHEST
    root_width = math.sqrt(D)
    rotated = rotation / root_width
    panel = lax.all_gather(rotated, ("dp", "layer"), axis=0, tiled=True)
    section = lax.axis_index("layer")
    width = embeddings.shape[1]
    full_width = width * lax.axis_size("tensor")
    column_start = lax.axis_index("tensor") * width
    micro_rows = embeddings.shape[0] // MICRO
    section_layers = layer_weight.shape[0]
    steps_total = MICRO + lax.axis_size("layer") - 1

    def join_columns(shard):
        return lax.all_gather(shard, "tensor", axis=1, tiled=True)

    def run_section(hidden):
        records = []
        shard = None
        for level in range(section_layers):
            widened, normed = normalize(hidden)
            update = jnp.dot(normed, layer_weight[level], preferred_element_type=jnp.float32)
            own_part = lax.dynamic_slice_in_dim(widened, column_start, width, 1)
            shard = (own_part + update).astype(jnp.bfloat16)
            records.append(normed)
            if level + 1 < section_layers:
                hidden = join_columns(shard)
        return (shard, jnp.stack(records))

    def step_fn(step, carry):
        previous, records_all = carry
        position = step - section
        valid = (position >= 0) & (position < MICRO)
        slot_index = jnp.clip(position, 0, MICRO - 1)
        fresh = lax.dynamic_slice_in_dim(embeddings, slot_index * micro_rows, micro_rows, 0)
        incoming = jnp.where(section == 0, join_columns(fresh), previous)
        shard, records = run_section(incoming)
        current = lax.dynamic_slice_in_dim(records_all, slot_index, 1, 1)
        chosen = jnp.where(valid, records[:, None], current)
        records_all = lax.dynamic_update_slice_in_dim(records_all, chosen, slot_index, 1)
        passed = passed_along(join_columns(shard), "layer", 1)
        return (passed, records_all)

    start_state = jnp.zeros((micro_rows, full_width), jnp.bfloat16)
    records_zero = jnp.zeros((section_layers, MICRO, micro_rows, full_width), jnp.bfloat16)
    final_state, records_all = lax.fori_loop(0, steps_total, step_fn, (start_state, records_zero))
    activations = records_all.reshape(-1, full_width)
    projected = jnp.dot(activations.astype(jnp.float32), panel, precision=exact_mode)
    cubed = projected * projected * projected
    columns = activations.astype(jnp.float32)
    summed = lax.psum_scatter(
        lax.dot_general(columns, cubed, (((0,), (0,)), ((), ())), precision=exact_mode),
        ("dp", "layer"),
        scatter_dimension=0,
        tiled=True,
    )
    gradient = summed / (embeddings.shape[0] * lax.axis_size("dp"))
    cross = lax.dot_general(gradient, panel, (((1,), (1,)), ((), ())), precision=exact_mode)
    cross_rows = lax.psum(cross, "tensor")
    swapped = lax.all_to_all(cross_rows, ("dp", "layer"), split_axis=1, concat_axis=0, tiled=True)
    skew_rows = cross_rows - swapped.T
    square_total = lax.psum(jnp.sum(skew_rows * skew_rows), ("dp", "layer"))
    mean_square = square_total / (full_width * full_width)
    step_size = 0.5 / jnp.sqrt(full_width * (mean_square + 1e-06))
    first_product = jnp.dot(skew_rows, panel, precision=exact_mode)
    first_guess = rotated - step_size * first_product
    second_product = jnp.dot(
        skew_rows,
        lax.all_gather(first_guess, ("dp", "layer"), axis=0, tiled=True),
        precision=exact_mode,
    )
    refined = rotated - 0.5 * step_size * (first_product + second_product)
    return root_width * refined


def solution(mesh):
    return jax.shard_map(
        shards,
        mesh=mesh,
        in_specs=(P("dp", "tensor"), P("layer", None, "tensor"), P(("dp", "layer"), "tensor")),
        out_specs=P(("dp", "layer"), "tensor"),
        check_vma=False,
    )
```

profile of v0, /device:TPU:0, one launch (start us, length us, event | category | flops | bytes accessed | tf_op | source)
XLA Modules:
  0.0 1216.2 jit_solution(3677848573825620444)
XLA Ops:
  10.1 428.7 %while.17 = (s32[]{:T(128)}, bf16[32,4096]{1,0:T(8,128)(2,1)S(1)}, bf16[2,4,32,4096]{3,2,1,0:T(8,128)(2,1)S(1)}, pred[]{:T(512)}, s32[]{:T(128)}, /*index=5*/bf1...) while((s32[]{:T(128)}, bf16[32,4096]{1,0:T(8,128)(2,1)S(1)}, ...), condition=%wide.region_3.4_spmd, body=%wide.region_0.3_spmd.sunk | while | flops 541065280 | bytes 26151456 | solution.py:68
  11.0 15.6 %all_gather.38 = bf16[32,4096]{1,0:T(8,128)(2,1)S(1)} all-gather(bf16[32,1024]{1,0:T(8,128)(2,1)S(1)} %constant_dynamic-slice_fusion.4), channel_id=1, replica_groups=mesh['dp'=2,'layer'=4,'tensor'=4] {'tensor'}, dimensions={1}, use_global_device_ids=true | all-gather | bytes 327680 | tf_op jit(solution)/shard_map/while/body/eval_jaxpr/all_gather | solution.py:37
  31.9 14.4 %all_gather.39 = bf16[32,4096]{1,0:T(8,128)(2,1)S(1)} all-gather(bf16[32,1024]{1,0:T(8,128)(2,1)S(1)} %fusion.45), channel_id=1, replica_groups=mesh['dp'=2,'layer'=4,'tensor'=4] {'tensor'}, dimensions={1}, use_global_device_ids=true | all-gather | bytes 327680 | tf_op jit(solution)/shard_map/while/body/eval_jaxpr/all_gather | solution.py:37
  46.5 5.0 fusion.46
  51.5 15.1 %all_gather.40 = bf16[32,4096]{1,0:T(8,128)(2,1)} all-gather(bf16[32,1024]{1,0:T(8,128)(2,1)S(1)} %fusion.46), channel_id=1, replica_groups=mesh['dp'=2,'layer'=4,'tensor'=4] {'tensor'}, dimensions={1}, use_global_device_ids=true | all-gather | bytes 327680 | tf_op jit(solution)/shard_map/while/body/eval_jaxpr/all_gather | solution.py:37
  70.2 13.9 %all_gather.38 = bf16[32,4096]{1,0:T(8,128)(2,1)S(1)} all-gather(bf16[32,1024]{1,0:T(8,128)(2,1)S(1)} %constant_dynamic-slice_fusion.4), channel_id=1, replica_groups=mesh['dp'=2,'layer'=4,'tensor'=4] {'tensor'}, dimensions={1}, use_global_device_ids=true | all-gather | bytes 327680 | tf_op jit(solution)/shard_map/while/body/eval_jaxpr/all_gather | solution.py:37
  84.4 5.0 fusion.45
  89.4 13.9 %all_gather.39 = bf16[32,4096]{1,0:T(8,128)(2,1)S(1)} all-gather(bf16[32,1024]{1,0:T(8,128)(2,1)S(1)} %fusion.45), channel_id=1, replica_groups=mesh['dp'=2,'layer'=4,'tensor'=4] {'tensor'}, dimensions={1}, use_global_device_ids=true | all-gather | bytes 327680 | tf_op jit(solution)/shard_map/while/body/eval_jaxpr/all_gather | solution.py:37
  103.5 5.0 fusion.46
  108.5 15.2 %all_gather.40 = bf16[32,4096]{1,0:T(8,128)(2,1)} all-gather(bf16[32,1024]{1,0:T(8,128)(2,1)S(1)} %fusion.46), channel_id=1, replica_groups=mesh['dp'=2,'layer'=4,'tensor'=4] {'tensor'}, dimensions={1}, use_global_device_ids=true | all-gather | bytes 327680 | tf_op jit(solution)/shard_map/while/body/eval_jaxpr/all_gather | solution.py:37
  129.2 13.9 %all_gather.38 = bf16[32,4096]{1,0:T(8,128)(2,1)S(1)} all-gather(bf16[32,1024]{1,0:T(8,128)(2,1)S(1)} %constant_dynamic-slice_fusion.4), channel_id=1, replica_groups=mesh['dp'=2,'layer'=4,'tensor'=4] {'tensor'}, dimensions={1}, use_global_device_ids=true | all-gather | bytes 327680 | tf_op jit(solution)/shard_map/while/body/eval_jaxpr/all_gather | solution.py:37
  143.3 5.0 fusion.45
  148.3 14.0 %all_gather.39 = bf16[32,4096]{1,0:T(8,128)(2,1)S(1)} all-gather(bf16[32,1024]{1,0:T(8,128)(2,1)S(1)} %fusion.45), channel_id=1, replica_groups=mesh['dp'=2,'layer'=4,'tensor'=4] {'tensor'}, dimensions={1}, use_global_device_ids=true | all-gather | bytes 327680 | tf_op jit(solution)/shard_map/while/body/eval_jaxpr/all_gather | solution.py:37
  162.5 5.0 fusion.46
  167.5 14.6 %all_gather.40 = bf16[32,4096]{1,0:T(8,128)(2,1)} all-gather(bf16[32,1024]{1,0:T(8,128)(2,1)S(1)} %fusion.46), channel_id=1, replica_groups=mesh['dp'=2,'layer'=4,'tensor'=4] {'tensor'}, dimensions={1}, use_global_device_ids=true | all-gather | bytes 327680 | tf_op jit(solution)/shard_map/while/body/eval_jaxpr/all_gather | solution.py:37
  182.2 7.4 collective-permute-start
  191.7 13.8 %all_gather.38 = bf16[32,4096]{1,0:T(8,128)(2,1)S(1)} all-gather(bf16[32,1024]{1,0:T(8,128)(2,1)S(1)} %constant_dynamic-slice_fusion.4), channel_id=1, replica_groups=mesh['dp'=2,'layer'=4,'tensor'=4] {'tensor'}, dimensions={1}, use_global_device_ids=true | all-gather | bytes 327680 | tf_op jit(solution)/shard_map/while/body/eval_jaxpr/all_gather | solution.py:37
  205.8 5.0 fusion.45
  210.8 13.8 %all_gather.39 = bf16[32,4096]{1,0:T(8,128)(2,1)S(1)} all-gather(bf16[32,1024]{1,0:T(8,128)(2,1)S(1)} %fusion.45), channel_id=1, replica_groups=mesh['dp'=2,'layer'=4,'tensor'=4] {'tensor'}, dimensions={1}, use_global_device_ids=true | all-gather | bytes 327680 | tf_op jit(solution)/shard_map/while/body/eval_jaxpr/all_gather | solution.py:37
  229.8 14.5 %all_gather.40 = bf16[32,4096]{1,0:T(8,128)(2,1)} all-gather(bf16[32,1024]{1,0:T(8,128)(2,1)S(1)} %fusion.46), channel_id=1, replica_groups=mesh['dp'=2,'layer'=4,'tensor'=4] {'tensor'}, dimensions={1}, use_global_device_ids=true | all-gather | bytes 327680 | tf_op jit(solution)/shard_map/while/body/eval_jaxpr/all_gather | solution.py:37
  244.3 6.7 collective-permute-start
  253.2 13.8 %all_gather.38 = bf16[32,4096]{1,0:T(8,128)(2,1)S(1)} all-gather(bf16[32,1024]{1,0:T(8,128)(2,1)S(1)} %constant_dynamic-slice_fusion.4), channel_id=1, replica_groups=mesh['dp'=2,'layer'=4,'tensor'=4] {'tensor'}, dimensions={1}, use_global_device_ids=true | all-gather | bytes 327680 | tf_op jit(solution)/shard_map/while/body/eval_jaxpr/all_gather | solution.py:37
  272.2 13.8 %all_gather.39 = bf16[32,4096]{1,0:T(8,128)(2,1)S(1)} all-gather(bf16[32,1024]{1,0:T(8,128)(2,1)S(1)} %fusion.45), channel_id=1, replica_groups=mesh['dp'=2,'layer'=4,'tensor'=4] {'tensor'}, dimensions={1}, use_global_device_ids=true | all-gather | bytes 327680 | tf_op jit(solution)/shard_map/while/body/eval_jaxpr/all_gather | solution.py:37
  291.3 14.5 %all_gather.40 = bf16[32,4096]{1,0:T(8,128)(2,1)} all-gather(bf16[32,1024]{1,0:T(8,128)(2,1)S(1)} %fusion.46), channel_id=1, replica_groups=mesh['dp'=2,'layer'=4,'tensor'=4] {'tensor'}, dimensions={1}, use_global_device_ids=true | all-gather | bytes 327680 | tf_op jit(solution)/shard_map/while/body/eval_jaxpr/all_gather | solution.py:37
  305.8 7.3 collective-permute-start
  315.3 13.9 %all_gather.38 = bf16[32,4096]{1,0:T(8,128)(2,1)S(1)} all-gather(bf16[32,1024]{1,0:T(8,128)(2,1)S(1)} %constant_dynamic-slice_fusion.4), channel_id=1, replica_groups=mesh['dp'=2,'layer'=4,'tensor'=4] {'tensor'}, dimensions={1}, use_global_device_ids=true | all-gather | bytes 327680 | tf_op jit(solution)/shard_map/while/body/eval_jaxpr/all_gather | solution.py:37
  329.5 5.0 fusion.45
  334.5 13.8 %all_gather.39 = bf16[32,4096]{1,0:T(8,128)(2,1)S(1)} all-gather(bf16[32,1024]{1,0:T(8,128)(2,1)S(1)} %fusion.45), channel_id=1, replica_groups=mesh['dp'=2,'layer'=4,'tensor'=4] {'tensor'}, dimensions={1}, use_global_device_ids=true | all-gather | bytes 327680 | tf_op jit(solution)/shard_map/while/body/eval_jaxpr/all_gather | solution.py:37
  348.5 5.0 fusion.46
  353.5 14.5 %all_gather.40 = bf16[32,4096]{1,0:T(8,128)(2,1)} all-gather(bf16[32,1024]{1,0:T(8,128)(2,1)S(1)} %fusion.46), channel_id=1, replica_groups=mesh['dp'=2,'layer'=4,'tensor'=4] {'tensor'}, dimensions={1}, use_global_device_ids=true | all-gather | bytes 327680 | tf_op jit(solution)/shard_map/while/body/eval_jaxpr/all_gather | solution.py:37
  368.1 7.2 collective-permute-start
  377.5 13.9 %all_gather.38 = bf16[32,4096]{1,0:T(8,128)(2,1)S(1)} all-gather(bf16[32,1024]{1,0:T(8,128)(2,1)S(1)} %constant_dynamic-slice_fusion.4), channel_id=1, replica_groups=mesh['dp'=2,'layer'=4,'tensor'=4] {'tensor'}, dimensions={1}, use_global_device_ids=true | all-gather | bytes 327680 | tf_op jit(solution)/shard_map/while/body/eval_jaxpr/all_gather | solution.py:37
  396.7 13.8 %all_gather.39 = bf16[32,4096]{1,0:T(8,128)(2,1)S(1)} all-gather(bf16[32,1024]{1,0:T(8,128)(2,1)S(1)} %fusion.45), channel_id=1, replica_groups=mesh['dp'=2,'layer'=4,'tensor'=4] {'tensor'}, dimensions={1}, use_global_device_ids=true | all-gather | bytes 327680 | tf_op jit(solution)/shard_map/while/body/eval_jaxpr/all_gather | solution.py:37
  415.7 14.5 %all_gather.40 = bf16[32,4096]{1,0:T(8,128)(2,1)} all-gather(bf16[32,1024]{1,0:T(8,128)(2,1)S(1)} %fusion.46), channel_id=1, replica_groups=mesh['dp'=2,'layer'=4,'tensor'=4] {'tensor'}, dimensions={1}, use_global_device_ids=true | all-gather | bytes 327680 | tf_op jit(solution)/shard_map/while/body/eval_jaxpr/all_gather | solution.py:37
  430.2 7.2 collective-permute-start
  438.8 12.0 fusion.29
  450.8 10.4 fusion.25
  461.4 131.6 %reduce-scatter.2.cloned.1.call-done = f32[512,1024]{1,0:T(8,128)} async-done(((f32[4096,1024]{1,0:T(8,128)}), f32[512,1024]{1,0:T(8,128)}) %reduce-scatter.2.cloned.1.call-update) | async-done | bytes 2097168 | tf_op jit(solution)/shard_map/reduce_scatter | solution.py:73
  593.0 31.8 %fusion.23 = f32[512,4096]{1,0:T(8,128)} fusion(f32[4096,1024]{1,0:T(8,128)} %all-gather.3.cloned.1.call-done, f32[512,1024]{1,0:T(8,128)} %reduce-scatter.2.cloned.1.call-done), kind=kOutput, calls=%fused_computation.29 | convolution fusion | flops 25770328064 | bytes 27262976 | tf_op jit(solution)/shard_map/dot_general | solution.py:80
  624.9 290.9 %all-reduce.2.cloned.1.call-done = f32[512,4096]{1,0:T(8,128)} async-done(((f32[512,4096]{1,0:T(8,128)}), f32[512,4096]{1,0:T(8,128)}) %all-reduce.2.cloned.1.call-update) | async-done | bytes 8388624 | tf_op jit(solution)/shard_map/psum | solution.py:81
  915.8 9.0 copy.10
  924.8 100.4 %all_to_all.19 = f32[512,8,512]{0,2,1:T(8,128)} all-to-all(f32[512,8,512]{0,2,1:T(8,128)} %bitcast.73), channel_id=1, replica_groups=mesh['dp'=2,'layer'=4,'tensor'=4] {'dp','layer'}, dimensions={1} | all-to-all | bytes 16777216 | tf_op jit(solution)/shard_map/all_to_all | solution.py:82
  1025.2 8.2 copy.14
  1033.4 6.3 multiply_reduce_fusion.2
  1039.7 13.2 %psum.15 = f32[]{:T(128)} all-reduce(f32[]{:T(128)} %multiply_reduce_fusion.2), channel_id=1, replica_groups=mesh['dp'=2,'layer'=4,'tensor'=4] {'dp','layer'}, use_global_device_ids=true, to_apply=%region_7.8 | all-reduce | flops 1 | bytes 8 | tf_op jit(solution)/shard_map/psum | solution.py:84
  1053.6 33.4 %multiply_subtract_fusion = (f32[512,1024]{1,0:T(8,128)}, f32[512,1024]{1,0:T(8,128)}) fusion(f32[]{:T(128)S(6)} %div.29, f32[512,1024]{1,0:T(8,128)S(1)} %copy-done, f32[4096,1024]{1,0:T(8,128)} %all-gather.3.cloned.1.call-done, f32[512,4096]{1,0:T(8,128)} %all-reduce.2.cloned.1.call-done, f32[4096,512]{0,1:T(8,128)} %bitcast.68), kind=kOutput, calls=%fused_computation.28 | convolution fusion | flops 25773473792 | bytes 39845892 | tf_op jit(solution)/shard_map/dot_general | solution.py:87
  1087.0 88.1 %all-gather.5.cloned.1.call-done = f32[4096,1024]{1,0:T(8,128)} async-done(((f32[512,1024]{1,0:T(8,128)}), f32[4096,1024]{1,0:T(8,128)}) %all-gather.5.cloned.1.call-update) | async-done | bytes 16777232 | tf_op jit(solution)/shard_map/all_gather | solution.py:91
  1175.1 34.5 %subtract_multiply_fusion = f32[512,1024]{1,0:T(8,128)} fusion(f32[512,1024]{1,0:T(8,128)} %get-tuple-element.203, f32[4096,1024]{1,0:T(8,128)} %all-gather.5.cloned.1.call-done, f32[]{:T(128)S(6)} %mul.119, f32[512,1024]{1,0:T(8,128)S(1)} %copy-done, f32[512,4096]{1,0:T(8,128)} %all-reduce.2.cloned.1.call-done, f32[4096,512]{0,1:T(8,128)} %bitcast.69), kind=kOutput, calls=%fused_computation.27 | convolution fusion | flops 25774522368 | bytes 39845892 | tf_op jit(solution)/shard_map/dot_general | solution.py:89
  (111 shorter events, 56.7 us)
Async XLA Ops:
  6.5 432.3 %all-gather.3.cloned.1.call-start = ((), (), s32[]{:S(2)}) async-start(), calls=%async_computation.2 | async-start | bytes 18874368 | tf_op jit(solution)/shard_map/all_gather | solution.py:27
  9.8 583.2 %reduce-scatter.2.cloned.1.call-start = ((), (), s32[]{:S(2)}) async-start(), calls=%async_computation.3 | async-start | bytes 18874368 | tf_op jit(solution)/shard_map/reduce_scatter | solution.py:73
  66.7 2.7 collective-permute-start
  123.7 4.6 collective-permute-start
  182.2 8.7 collective-permute-start
  244.3 8.0 collective-permute-start
  305.8 8.7 collective-permute-start
  368.1 8.6 collective-permute-start
  430.2 8.6 collective-permute-start
  461.2 454.6 %all-reduce.2.cloned.1.call-start = ((), (), s32[]{:S(2)}) async-start(), calls=%async_computation.4 | async-start | bytes 16777216 | tf_op jit(solution)/shard_map/psum | solution.py:81
  624.8 550.3 %all-gather.5.cloned.1.call-start = ((), (), s32[]{:S(2)}) async-start(), calls=%async_computation.5 | async-start | bytes 18874368 | tf_op jit(solution)/shard_map/all_gather | solution.py:91
  924.8 108.6 %slice-start = ((s8[8388608]{0:T(1024)(128)(4,1)}), s8[4194304]{0:T(1024)(128)(4,1)S(1)}, s32[]{:S(2)}) async-start(s8[8388608]{0:T(1024)(128)(4,1)} %bitcast.65), calls=%async_computation.6 | async-start | bytes 8388608
  1025.2 8.2 slice-start.1
  1033.4 20.2 %copy-start = (f32[512,1024]{1,0:T(8,128)S(1)}, f32[512,1024]{1,0:T(8,128)}, u32[]{:S(2)}) copy-start(f32[512,1024]{1,0:T(8,128)} %param.7) | copy-start | bytes 6291460
Sparse Core Ops, SparseCore 0:
  9.9 92.6 all-gather.2
  461.3 131.6 reduce-scatter.1
  625.0 290.8 all-reduce.1
  1087.1 87.9 all-gather.4
where the time goes:
time: 1220 us
  waiting for transfers between devices  517 us (42%)
  blocking collectives  413 us (34%)
  matrix products  192 us (16%)
  starting transfers between devices  40.8 us (3%)
  local copies, waits for them, and re-layouts  23.7 us (2%)
  other arithmetic  15.3 us (1%)
  between operations  13.9 us (1%)
    all_gather x21, blocking collectives, join_columns(): return lax.all_gather(shard, 'tensor', axis=1, tiled=True)  299 us
    psum x1, waiting for transfers between devices, shards(): cross_rows = lax.psum(cross, 'tensor')  291 us
    reduce_scatter x1, waiting for transfers between devices, shards(): lax.psum_scatter(lax.dot_general(columns, cubed, (((0,), (0,)), ((), ()))...  132 us
    all_to_all x1, blocking collectives, shards(): lax.all_to_all(cross_rows, ('dp', 'layer'), split_axis=1, concat_axis=0,...  100 us
    all_gather x1, waiting for transfers between devices, shards(): lax.all_gather(first_guess, ('dp', 'layer'), axis=0, tiled=True)  88.1 us
    dot_general x14, matrix products, run_section(): jnp.dot(normed, layer_weight[level], preferred_element_type=jnp.float32)  69.8 us
    ppermute x7, starting transfers between devices, passed_along(): lax.ppermute(value, axis, [(source, source + steps) for source in range(i...  40.5 us
    dot_general x1, matrix products, shards(): jnp.dot(skew_rows, lax.all_gather(first_guess, ('dp', 'layer'), axis=0, t...  34.5 us
  transfers between devices with their start and end apart: 11, of which 10 were waited for; matrix products, arithmetic and copies ran while one was open for 7% of the time, Pallas kernels for 0%

commit v1 on v0

--- a/solution.py
+++ b/solution.py
@@ -6,6 +6,19 @@
 
 D = 4096
 MICRO = 4
+
+
+def ring_gather(shard, axis, dim):
+    ways = lax.axis_size(axis)
+    up = [(d, (d + 1) % ways) for d in range(ways)]
+    down = [(d, (d - 1) % ways) for d in range(ways)]
+    earlier, later = ([shard], [shard])
+    for _ in range(ways // 2):
+        earlier.append(lax.ppermute(earlier[-1], axis, up))
+    for _ in range((ways - 1) // 2):
+        later.append(lax.ppermute(later[-1], axis, down))
+    line = jnp.concatenate([*earlier[::-1], *later[1:]], axis=dim)
+    return jnp.roll(line, (lax.axis_index(axis) - ways // 2) * shard.shape[dim], axis=dim)
 
 
 def passed_along(value, axis, steps):
@@ -34,7 +47,7 @@
     steps_total = MICRO + lax.axis_size("layer") - 1
 
     def join_columns(shard):
-        return lax.all_gather(shard, "tensor", axis=1, tiled=True)
+        return ring_gather(shard, "tensor", 1)
 
     def run_section(hidden):
         records = []

time: 1220 us -> 1190 us (0.975)
  blocking collectives: 413 us -> 114 us
  waiting for transfers between devices: 517 us -> 688 us
  starting transfers between devices: 40.8 us -> 122 us
  other arithmetic: 15.3 us -> 30.6 us
    all_gather x21 -> x0, blocking collectives: 299 us -> none  [join_columns(): return lax.all_gather(shard, 'tensor', axis=1, tiled=True)]
    ppermute x0 -> x63, waiting for transfers between devices: none -> 176 us  [the longest x42 175 us: ring_gather(): earlier.append(lax.ppermute(earlier[-1], axis, up))]
    ppermute x0 -> x63, starting transfers between devices: none -> 82.6 us  [the longest x21 78.7 us: ring_gather(): later.append(lax.ppermute(later[-1], axis, down))]
  transfers between devices with their start and end apart: 11 -> 74, of which waited for: 10 -> 53; matrix products, arithmetic and copies ran while one was open for 7% -> 8% of each run, Pallas kernels for 0% -> 0%
where the time goes in v1:
time: 1190 us
  waiting for transfers between devices  688 us (58%)
  matrix products  193 us (16%)
  starting transfers between devices  122 us (10%)
  blocking collectives  114 us (10%)
  other arithmetic  30.6 us (3%)
  local copies, waits for them, and re-layouts  23.6 us (2%)
  between operations  14.1 us (1%)
    psum x1, waiting for transfers between devices, shards(): cross_rows = lax.psum(cross, 'tensor')  291 us
    ppermute x42, waiting for transfers between devices, ring_gather(): earlier.append(lax.ppermute(earlier[-1], axis, up))  175 us
    reduce_scatter x1, waiting for transfers between devices, shards(): lax.psum_scatter(lax.dot_general(columns, cubed, (((0,), (0,)), ((), ()))...  126 us
    all_to_all x1, blocking collectives, shards(): lax.all_to_all(cross_rows, ('dp', 'layer'), split_axis=1, concat_axis=0,...  101 us
    all_gather x1, waiting for transfers between devices, shards(): lax.all_gather(first_guess, ('dp', 'layer'), axis=0, tiled=True)  88.1 us
    ppermute x21, starting transfers between devices, ring_gather(): later.append(lax.ppermute(later[-1], axis, down))  78.7 us
    dot_general x14, matrix products, run_section(): jnp.dot(normed, layer_weight[level], preferred_element_type=jnp.float32)  69.9 us
    ppermute x7, starting transfers between devices, passed_along(): lax.ppermute(value, axis, [(source, source + steps) for source in range(i...  39.8 us
  transfers between devices with their start and end apart: 74, of which 53 were waited for; matrix products, arithmetic and copies ran while one was open for 8% of the time, Pallas kernels for 0%

profile of v1, /device:TPU:0, one launch (start us, length us, event | category | flops | bytes accessed | tf_op | source)
XLA Modules:
  0.0 1185.8 jit_solution(18088958684086828137)
XLA Ops:
  10.1 402.8 %while.17 = (s32[]{:T(128)}, bf16[32,4096]{1,0:T(8,128)(2,1)S(1)}, bf16[2,4,32,4096]{3,2,1,0:T(8,128)(2,1)S(1)}, pred[]{:T(512)}, s32[]{:T(128)}, /*index=5*/bf1...) while((s32[]{:T(128)}, bf16[32,4096]{1,0:T(8,128)(2,1)S(1)}, ...), condition=%wide.region_3.5_spmd, body=%wide.region_0.4_spmd.sunk | while | flops 546439296 | bytes 28315532 | solution.py:81
  19.0 5.5 collective-permute-done.2
  36.6 6.0 collective-permute-done.5
  43.5 5.0 fusion.73
  55.4 5.9 collective-permute-done.7
  71.5 6.2 collective-permute-done.2
  89.8 6.1 collective-permute-done.5
  96.8 5.0 fusion.73
  108.1 5.9 collective-permute-done.7
  127.8 6.1 collective-permute-done.2
  134.8 5.0 fusion.72
  146.0 6.1 collective-permute-done.5
  153.1 5.0 fusion.73
  164.3 6.0 collective-permute-done.7
  171.1 7.3 collective-permute-start.9
  186.5 6.1 collective-permute-done.2
  193.5 5.0 fusion.72
  204.6 6.0 collective-permute-done.5
  222.8 6.3 collective-permute-done.7
  230.0 7.0 collective-permute-start.9
  245.0 6.1 collective-permute-done.2
  252.0 5.0 fusion.72
  263.1 6.0 collective-permute-done.5
  281.3 6.6 collective-permute-done.7
  288.8 6.9 collective-permute-start.9
  303.7 6.1 collective-permute-done.2
  310.7 5.0 fusion.72
  321.9 6.1 collective-permute-done.5
  328.9 5.0 fusion.73
  340.1 6.6 collective-permute-done.7
  347.5 6.0 collective-permute-start.9
  361.6 6.1 collective-permute-done.2
  379.8 6.0 collective-permute-done.5
  398.0 6.6 collective-permute-done.7
  405.4 6.4 collective-permute-start.9
  412.9 12.0 %fusion.55 = f32[256,1024]{1,0:T(8,128)S(1)} fusion(bf16[256,4096]{1,0:T(8,128)(2,1)S(1)} %bitcast.70, f32[4096,1024]{1,0:T(8,128)} %all-gather.3.cloned.1.call-done), kind=kOutput, calls=%fused_computation.84 | convolution fusion | flops 12884901888 | bytes 19922944 | tf_op jit(solution)/shard_map/dot_general | solution.py:83
  424.9 10.9 fusion.49
  435.8 126.4 %reduce-scatter.2.cloned.1.call-done = f32[512,1024]{1,0:T(8,128)} async-done(((f32[4096,1024]{1,0:T(8,128)}), f32[512,1024]{1,0:T(8,128)}) %reduce-scatter.2.cloned.1.call-update) | async-done | bytes 2097168 | tf_op jit(solution)/shard_map/reduce_scatter | solution.py:86
  562.2 31.8 %fusion.47 = f32[512,4096]{1,0:T(8,128)} fusion(f32[4096,1024]{1,0:T(8,128)} %all-gather.3.cloned.1.call-done, f32[512,1024]{1,0:T(8,128)} %reduce-scatter.2.cloned.1.call-done), kind=kOutput, calls=%fused_computation.76 | convolution fusion | flops 25770328064 | bytes 27262976 | tf_op jit(solution)/shard_map/dot_general | solution.py:93
  594.1 290.9 %all-reduce.2.cloned.1.call-done = f32[512,4096]{1,0:T(8,128)} async-done(((f32[512,4096]{1,0:T(8,128)}), f32[512,4096]{1,0:T(8,128)}) %all-reduce.2.cloned.1.call-update) | async-done | bytes 8388624 | tf_op jit(solution)/shard_map/psum | solution.py:94
  885.0 9.0 copy.10
  894.1 100.6 %all_to_all.19 = f32[512,8,512]{0,2,1:T(8,128)} all-to-all(f32[512,8,512]{0,2,1:T(8,128)} %bitcast.73), channel_id=1, replica_groups=mesh['dp'=2,'layer'=4,'tensor'=4] {'dp','layer'}, dimensions={1} | all-to-all | bytes 16777216 | tf_op jit(solution)/shard_map/all_to_all | solution.py:95
  994.6 8.2 copy.14
  1002.9 6.3 multiply_reduce_fusion.2
  1009.2 13.0 %psum.15 = f32[]{:T(128)} all-reduce(f32[]{:T(128)} %multiply_reduce_fusion.2), channel_id=1, replica_groups=mesh['dp'=2,'layer'=4,'tensor'=4] {'dp','layer'}, use_global_device_ids=true, to_apply=%region_7.9 | all-reduce | flops 1 | bytes 8 | tf_op jit(solution)/shard_map/psum | solution.py:97
  1022.8 33.4 %multiply_subtract_fusion = (f32[512,1024]{1,0:T(8,128)}, f32[512,1024]{1,0:T(8,128)}) fusion(f32[]{:T(128)S(6)} %div.29, f32[512,1024]{1,0:T(8,128)S(1)} %copy-done, f32[4096,1024]{1,0:T(8,128)} %all-gather.3.cloned.1.call-done, f32[512,4096]{1,0:T(8,128)} %all-reduce.2.cloned.1.call-done, f32[4096,512]{0,1:T(8,128)} %bitcast.68), kind=kOutput, calls=%fused_computation.75 | convolution fusion | flops 25773473792 | bytes 39845892 | tf_op jit(solution)/shard_map/dot_general | solution.py:100
  1056.2 88.1 %all-gather.5.cloned.1.call-done = f32[4096,1024]{1,0:T(8,128)} async-done(((f32[512,1024]{1,0:T(8,128)}), f32[4096,1024]{1,0:T(8,128)}) %all-gather.5.cloned.1.call-update) | async-done | bytes 16777232 | tf_op jit(solution)/shard_map/all_gather | solution.py:104
  1144.4 34.7 %subtract_multiply_fusion = f32[512,1024]{1,0:T(8,128)} fusion(f32[512,1024]{1,0:T(8,128)} %get-tuple-element.214, f32[4096,1024]{1,0:T(8,128)} %all-gather.5.cloned.1.call-done, f32[]{:T(128)S(6)} %mul.138, f32[512,1024]{1,0:T(8,128)S(1)} %copy-done, f32[512,4096]{1,0:T(8,128)} %all-reduce.2.cloned.1.call-done, f32[4096,512]{0,1:T(8,128)} %bitcast.69), kind=kOutput, calls=%fused_computation.74 | convolution fusion | flops 25774522368 | bytes 39845892 | tf_op jit(solution)/shard_map/dot_general | solution.py:102
  (209 shorter events, 203.9 us)
Async XLA Ops:
  6.5 406.4 %all-gather.3.cloned.1.call-start = ((), (), s32[]{:S(2)}) async-start(), calls=%async_computation.2 | async-start | bytes 18874368 | tf_op jit(solution)/shard_map/all_gather | solution.py:40
  9.8 552.5 %reduce-scatter.2.cloned.1.call-start = ((), (), s32[]{:S(2)}) async-start(), calls=%async_computation.3 | async-start | bytes 18874368 | tf_op jit(solution)/shard_map/reduce_scatter | solution.py:86
  11.0 7.4 collective-permute-start.1
  30.4 6.1 collective-permute-start.4
  30.5 6.1 collective-permute-start.3
  48.5 6.8 collective-permute-start.6
  48.7 6.7 collective-permute-start.8
  65.5 6.1 collective-permute-start
  71.5 6.2 collective-permute-start.2
  83.6 6.1 collective-permute-start.4
  83.7 6.1 collective-permute-start.3
  89.7 6.2 collective-permute-start.5
  101.8 6.1 collective-permute-start.6
  114.8 6.1 collective-permute-start.9
  121.8 6.1 collective-permute-start
  139.8 6.1 collective-permute-start.4
  139.9 6.1 collective-permute-start.3
  146.0 6.2 collective-permute-start.5
  158.1 6.1 collective-permute-start.6
  164.2 6.1 collective-permute-start.7
  171.1 8.4 collective-permute-start.9
  198.5 6.1 collective-permute-start.4
  198.5 6.1 collective-permute-start.3
  204.6 6.1 collective-permute-start.5
  216.6 6.1 collective-permute-start.6
  222.7 6.5 collective-permute-start.7
  230.0 8.1 collective-permute-start.9
  257.0 6.1 collective-permute-start.4
  257.0 6.1 collective-permute-start.3
  263.1 6.1 collective-permute-start.5
  275.1 6.1 collective-permute-start.6
  281.2 6.8 collective-permute-start.7
  288.8 8.0 collective-permute-start.9
  303.7 6.1 collective-permute-start.2
  315.7 6.1 collective-permute-start.4
  315.8 6.1 collective-permute-start.3
  321.8 6.1 collective-permute-start.5
  333.9 6.1 collective-permute-start.6
  340.0 6.7 collective-permute-start.7
  347.5 7.1 collective-permute-start.9
  373.6 6.1 collective-permute-start.4
  373.6 6.1 collective-permute-start.3
  379.7 6.1 collective-permute-start.5
  391.7 6.1 collective-permute-start.6
  397.8 6.8 collective-permute-start.7
  405.4 7.5 collective-permute-start.9
  435.8 449.3 %all-reduce.2.cloned.1.call-start = ((), (), s32[]{:S(2)}) async-start(), calls=%async_computation.4 | async-start | bytes 16777216 | tf_op jit(solution)/shard_map/psum | solution.py:94
  594.1 550.3 %all-gather.5.cloned.1.call-start = ((), (), s32[]{:S(2)}) async-start(), calls=%async_computation.5 | async-start | bytes 18874368 | tf_op jit(solution)/shard_map/all_gather | solution.py:104
  (29 other events, 289.9 us)
Sparse Core Ops, SparseCore 0:
  9.9 92.5 all-gather.2
  435.9 126.2 reduce-scatter.1
  594.2 290.8 all-reduce.1
  1056.4 87.9 all-gather.4
